TPU v7x, 32 devices: a whole 2x2x4 slice. The times are simulated.
32 devices in a mesh: grp: 2 (over y), wide: 16 (over z, x, core).
Axes of the slice: x: 2, y: 2, z: 4, core: 2. Of those that a mesh axis runs over, the one named last changes fastest.
Arguments:
- activations: bfloat16 [2, 1024, 4096], P('grp', 'wide'), parts along dimension 0, may hold values from -6 to 6
- output_grads: bfloat16 [2, 1024, 4096], P('grp', None, 'wide'), parts along dimension 0, may hold values from -0.1875 to 0.1875
- token_ids: int32 [2, 1024], P('grp'), parts along dimension 0, may hold values from 0 to 128255, as said below
- row_signs: int32 [4096], replicated, may hold values from -1 to 1, as said below
- column_signs: int32 [4096], replicated, may hold values from -1 to 1, as said below
- kept_blocks: int32 [8192], P('wide'), may hold values from 0 to 131071, as said below
- queries: bfloat16 [256, 1048576], P(None, 'wide'), may hold values from -0.0078125 to 0.0078125
Outputs:
- sketches: bfloat16 [2, 1048576], P('grp', 'wide'), parts along dimension 0
- scores: float32 [256, 2], P('wide', 'grp'), parts along dimension 1
There are 2 independent parts, one for each index of `grp`. A program takes and returns all parts, laid end to end along the dimension named above; an argument that names none is the same for every part. Nothing has to cross between parts.
Inputs may be any that keep to these rules, and one draw needn't show every extreme that they name: `token_ids`: id 0 marks padding. Each sequence ends with one run of one or more padding ids, and 512 or more of its ids are 1 or more. `row_signs`: every entry is +1 or -1. `column_signs`: every entry is +1 or -1. `kept_blocks`: A block number b names column b // 32 and rows (b % 32) * 128 up to (b % 32 + 1) * 128 - 1 of a sequence's projected matrix. For every d, entries d * 512 up to (d + 1) * 512 - 1 are distinct and name columns d * 256 up to (d + 1) * 256 - 1.
All inputs are finite; a program needn't handle non-finite values.
Results may differ from a plain program's by a relative error of at most 0.006.
Values may be sent and summed in bfloat16 or wider, within the bound.
A program may use at most 256 MiB of HBM per device.

v0:
```python
import jax
import jax.numpy as jnp
from jax import lax
from jax.sharding import PartitionSpec as P

ROWBLK = 128


def sign_table(bit_count):
    length = 2**bit_count
    indices = jnp.arange(length, dtype=jnp.int32)
    common = jnp.bitwise_and(indices[:, None], indices[None, :])
    parity = jnp.zeros((length, length), jnp.int32)
    for position in range(bit_count):
        parity = parity + jnp.bitwise_and(jnp.right_shift(common, position), 1)
    signs = 1 - 2 * jnp.bitwise_and(parity, 1)
    return (signs.astype(jnp.float32) * length ** (-0.5)).astype(jnp.bfloat16)


def hadamard_table(order_size):
    total_bits = order_size.bit_length() - 1
    low_bits = total_bits // 2
    high_table = sign_table(total_bits - low_bits)
    low_table = sign_table(low_bits)
    high_table, low_table = lax.optimization_barrier((high_table, low_table))
    return (high_table[:, None, :, None] * low_table[None, :, None, :]).reshape(
        order_size, order_size
    )


def per_device(activations, output_grads, token_ids, row_signs, column_signs, kept_blocks, queries):
    model_width = column_signs.shape[0]
    hadamard = hadamard_table(model_width)
    row_blocks = model_width // ROWBLK
    column_sign = column_signs.astype(jnp.bfloat16)
    row_sign = row_signs.astype(jnp.bfloat16)
    weight = (token_ids != 0).astype(jnp.bfloat16)
    columns_dev = output_grads.shape[2]
    device = lax.axis_index("wide")
    local_blocks = kept_blocks - device * (columns_dev * row_blocks)
    turned = jnp.einsum(
        "stj,jk->stk",
        activations * column_sign[None, None, :],
        hadamard,
        preferred_element_type=jnp.float32,
    ).astype(jnp.bfloat16)
    columns = lax.all_to_all(turned, "wide", split_axis=2, concat_axis=1, tiled=True)
    weighted = columns * weight[:, :, None]
    half_turned = jnp.einsum(
        "stc,sti->sci",
        weighted,
        lax.all_gather(output_grads, "wide", axis=2, tiled=True),
        preferred_element_type=jnp.float32,
    ).astype(jnp.bfloat16)
    signed = half_turned * row_sign[None, None, :]
    projected = jnp.einsum("scj,ji->sci", signed, hadamard, preferred_element_type=jnp.float32)
    items = projected.shape[0]
    block_rows = projected.reshape(items, projected.shape[1] * row_blocks, ROWBLK)
    picked = jnp.take(block_rows, local_blocks, axis=1)
    sketches = picked.reshape(items, picked.shape[1] * ROWBLK).astype(jnp.bfloat16)
    scores = lax.psum_scatter(
        jnp.einsum("qc,sc->qs", queries, sketches, preferred_element_type=jnp.float32),
        "wide",
        scatter_dimension=0,
        tiled=True,
    )
    return (sketches, scores)


def solution(mesh):
    placed = (
        P("grp", "wide", None),
        P("grp", None, "wide"),
        P("grp", None),
        P(),
        P(),
        P("wide"),
        P(None, "wide"),
    )
    return jax.shard_map(
        per_device,
        mesh=mesh,
        in_specs=placed,
        out_specs=(P("grp", "wide"), P("wide", "grp")),
        check_vma=False,
    )
```

profile of v0, /device:TPU:0, one launch (start us, length us, event | category | flops | bytes accessed | tf_op | source)
XLA Modules:
  0.0 292.9 jit_solution(1452810544550997973)
XLA Ops:
  7.2 0.0 all-gather.2.cloned.1.call-start
  7.2 0.7 all-gather.2.cloned.1.call-update
  7.9 21.2 %broadcast_multiply_fusion = bf16[64,64,64,64]{3,2,1,0:T(8,128)(2,1)} fusion(bf16[64,64]{1,0:T(8,128)(2,1)S(1)} %multiply_convert_fusion), kind=kLoop, calls=%fused_computation.1 | loop fusion | flops 16777216 | bytes 33562624 | tf_op jit(solution)/shard_map/mul | solution.py:26
  29.1 0.0 copy-start.1
  29.1 0.0 copy-start
  29.1 87.2 %mul.83 = bf16[4096,4096]{1,0:T(8,128)(2,1)} reshape(bf16[64,64,64,64]{3,2,1,0:T(8,128)(2,1)} %broadcast_multiply_fusion) | data formatting | bytes 67108864 | tf_op jit(solution)/shard_map/mul | solution.py:26
  116.3 0.0 copy-done.1
  116.3 0.0 copy-done
  116.3 13.6 %fusion.8 = bf16[1,64,4096]{2,1,0:T(8,128)(2,1)S(1)} fusion(bf16[4096,4096]{1,0:T(8,128)(2,1)} %mul.83, bf16[1,64,4096]{2,1,0:T(8,128)(2,1)S(1)} %copy-done, bf16[4096]{0:T(1024)(128)(2,1)S(1)} %convert_element_type.43), kind=kOutput, calls=%fused_computation.7 | convolution fusion | flops 2148007936 | bytes 34611200 | tf_op jit(solution)/shard_map/stj,jk->stk/dot_general | solution.py:41
  130.0 0.0 copy-start.3
  130.0 0.0 copy-start.2
  130.0 0.0 copy-start.4
  130.0 2.8 copy.12
  132.8 0.5 broadcast.80
  133.3 22.4 %reduce.2 = bf16[4096,64]{1,0:T(8,128)(2,1)S(1)} reduce(bf16[4096,1,64]{2,1,0:T(2,128)(2,1)S(1)} %bitcast.56, bf16[]{:T(256)} %broadcast.80), dimensions={1}, to_apply=%bitcast.47.reduce_sub_computation | reduce | bytes 1048578
  155.7 1.5 reshape.131
  157.2 7.4 %all-to-all-start = ((bf16[16,2,8192]{2,1,0:T(2,128)(2,1)}), bf16[16,2,8192]{2,1,0:T(2,128)(2,1)S(1)}, u32[]{:S(2)}, u32[]{:S(2)}) async-start(bf16[16,2,8192]{2,1,0:T(2,128)(2,1)} %reshape.131), calls=%async_computation | async-start | bytes 1048576 | tf_op jit(solution)/shard_map/all_to_all | solution.py:47
  164.7 0.2 reduce-scatter.4.cloned.1.call-start
  164.9 0.0 copy-done.3
  164.9 0.1 reshape.111
  165.0 0.1 copy.14
  165.1 0.0 copy-done.2
  165.1 0.0 copy-done.4
  165.2 0.1 broadcast_bitcast_fusion
  165.3 13.6 %all-to-all-done = bf16[16,2,8192]{2,1,0:T(2,128)(2,1)S(1)} async-done(((bf16[16,2,8192]{2,1,0:T(2,128)(2,1)}), bf16[16,2,8192]{2,1,0:T(2,128)(2,1)S(1)}, u32[]{:S(2)}, u32[]{:S(2)}) %all-to-all-start) | async-done | bytes 524320 | tf_op jit(solution)/shard_map/all_to_all | solution.py:47
  178.9 1.2 reshape.132
  180.2 2.3 copy.13
  182.5 0.1 copy.19
  182.6 0.2 fusion.13
  182.8 0.2 copy.15
  182.9 0.0 all-gather.2.cloned.1.call-done
  183.0 22.9 %fusion.10 = f32[256,4096]{1,0:T(8,128)} fusion(bf16[4096,4096]{1,0:T(8,128)(2,1)} %mul.83, bf16[1024,256]{1,0:T(8,128)(2,1)S(1)} %bitcast.60, bf16[1,1024,4096]{2,1,0:T(8,128)(2,1)} %all-gather.2.cloned.1.call-done, bf16[4096]{0:T(1024)(128)(2,1)S(1)} %convert_element_type.49), kind=kOutput, calls=%fused_computation.8 | convolution fusion | flops 10739515392 | bytes 46669824 | tf_op jit(solution)/shard_map/scj,ji->sci/dot_general | solution.py:56
  205.9 4.9 %reshape.112 = f32[8192,128]{1,0:T(8,128)} reshape(f32[256,4096]{1,0:T(8,128)} %fusion.10) | data formatting | bytes 8388608 | tf_op jit(solution)/shard_map/reshape | solution.py:58
  210.8 3.2 %gather_fusion = f32[512,128]{1,0:T(8,128)S(1)} fusion(f32[8192,128]{1,0:T(8,128)} %reshape.112, s32[1024]{0:T(1024)S(1)} %pad_clamp_fusion), kind=kCustom, calls=%fused_computation | custom fusion | bytes 526336 | tf_op jit(solution)/shard_map/jit(_take)/gather | solution.py:59
  214.1 0.1 fusion.17
  214.2 0.1 reshape.126
  214.3 15.1 %convolution_bitcast_fusion = f32[256,1]{1,0:T(8,128)} fusion(bf16[65536,1]{0,1:T(2,128)(2,1)S(1)} %reshape.126, bf16[256,65536]{1,0:T(8,128)(2,1)} %param.13), kind=kOutput, calls=%fused_computation.9 | convolution fusion | flops 33554432 | bytes 33686528 | tf_op jit(solution)/shard_map/qc,sc->qs/dot_general | solution.py:62
  229.4 0.0 reduce-scatter.4.cloned.1.call-update
  229.4 1.1 fusion.16
  230.5 54.3 %reduce-scatter.4.cloned.1.call-done = f32[16,1]{1,0:T(8,128)} async-done(((f32[256,1]{1,0:T(8,128)}), f32[16,1]{1,0:T(8,128)}) %reduce-scatter.4.cloned.1.call-update) | async-done | bytes 80
  284.8 1.3 copy.17
  (6 shorter events, 0.1 us)
Async XLA Ops:
  7.2 175.8 %all-gather.2.cloned.1.call-start = ((), (), s32[]{:S(2)}) async-start(), calls=%async_computation.2 | async-start | bytes 8912896 | tf_op jit(solution)/shard_map/all_gather | solution.py:52
  29.1 87.2 %copy-start.1 = (s32[4096]{0:T(1024)S(1)}, s32[4096]{0:T(1024)}, u32[]{:S(2)}) copy-start(s32[4096]{0:T(1024)} %param.11) | copy-start | bytes 49156
  29.1 87.2 %copy-start = (bf16[1,64,4096]{2,1,0:T(8,128)(2,1)S(1)}, bf16[1,64,4096]{2,1,0:T(8,128)(2,1)}, u32[]{:S(2)}) copy-start(bf16[1,64,4096]{2,1,0:T(8,128)(2,1)} %param.7) | copy-start | bytes 1572868
  130.0 34.9 %copy-start.3 = (s32[1,1024]{1,0:T(1,128)S(1)}, s32[1,1024]{1,0:T(1,128)}, u32[]{:S(2)}) copy-start(s32[1,1024]{1,0:T(1,128)} %param.9) | copy-start | bytes 12292
  130.0 35.2 %copy-start.2 = (s32[4096]{0:T(1024)S(1)}, s32[4096]{0:T(1024)}, u32[]{:S(2)}) copy-start(s32[4096]{0:T(1024)} %param.10) | copy-start | bytes 49156
  130.0 35.2 %copy-start.4 = (s32[512]{0:T(512)S(1)}, s32[512]{0:T(512)}, u32[]{:S(2)}) copy-start(s32[512]{0:T(512)} %param.12) | copy-start | bytes 6148
  157.2 21.7 %all-to-all-start = ((bf16[16,2,8192]{2,1,0:T(2,128)(2,1)}), bf16[16,2,8192]{2,1,0:T(2,128)(2,1)S(1)}, u32[]{:S(2)}, u32[]{:S(2)}) async-start(bf16[16,2,8192]{2,1,0:T(2,128)(2,1)} %reshape.131), calls=%async_computation | async-start | bytes 1048576 | tf_op jit(solution)/shard_map/all_to_all | solution.py:47
  164.7 120.1 %reduce-scatter.4.cloned.1.call-start = ((), (), s32[]{:S(2)}) async-start(), calls=%async_computation.3 | async-start | bytes 139264
Sparse Core Ops, SparseCore 0:
  10.1 80.4 all-gather.1
  229.6 55.1 reduce-scatter.3
where the time goes:
time: 296 us; the launch traced here: 293 us
  local copies, waits for them, and re-layouts  106 us (36%)
  waiting for transfers between devices  68.6 us (23%)
  matrix products  51.7 us (17%)
  other arithmetic  45.1 us (15%)
  between operations  14.2 us (5%)
  starting transfers between devices  7.7 us (3%)
    mul x1, local copies, waits for them, and re-layouts, hadamard_table(): high_table[:, None, :, None] * low_table[None, :, None, :]  87.2 us
    unnamed x3, waiting for transfers between devices  55 us
    dot_general x1, matrix products, per_device(): jnp.einsum('scj,ji->sci', signed, hadamard, preferred_element_type=jnp.fl...  22.9 us
    unnamed x1, other arithmetic  22.4 us
    mul x1, other arithmetic, hadamard_table(): high_table[:, None, :, None] * low_table[None, :, None, :]  21.2 us
    dot_general x1, matrix products, per_device(): jnp.einsum('qc,sc->qs', queries, sketches, preferred_element_type=jnp.flo...  15.1 us
    dot_general x1, matrix products, per_device(): jnp.einsum('stj,jk->stk', activations * column_sign[None, None, :], hadam...  13.6 us
    all_to_all x1, waiting for transfers between devices, per_device(): lax.all_to_all(turned, 'wide', split_axis=2, concat_axis=1, tiled=True)  13.6 us
  transfers between devices with their start and end apart: 3, of which 2 were waited for; matrix products, arithmetic and copies ran while one was open for 53% of the time, Pallas kernels for 0%

commit v1 on v0

--- a/solution.py
+++ b/solution.py
@@ -1,6 +1,10 @@
+import functools
+
 import jax
 import jax.numpy as jnp
 from jax import lax
+from jax.experimental import pallas as pl
+from jax.experimental.pallas import tpu as pltpu
 from jax.sharding import PartitionSpec as P
 
 ROWBLK = 128
@@ -28,7 +32,7 @@
     )
 
 
-def per_device(activations, output_grads, token_ids, row_signs, column_signs, kept_blocks, queries):
+def per_device_plain(activations, output_grads, token_ids, row_signs, column_signs, kept_blocks, queries):
     model_width = column_signs.shape[0]
     hadamard = hadamard_table(model_width)
     row_blocks = model_width // ROWBLK
@@ -67,6 +71,326 @@
     return (sketches, scores)
 
 
+def signs(size):
+    common = jnp.bitwise_and(
+        lax.broadcasted_iota(jnp.int32, (size, size), 0),
+        lax.broadcasted_iota(jnp.int32, (size, size), 1),
+    )
+    shift = 1
+    while shift < size:
+        common = jnp.bitwise_xor(common, jnp.right_shift(common, shift))
+        shift *= 2
+    return (1 - 2 * jnp.bitwise_and(common, 1)).astype(jnp.float32).astype(jnp.bfloat16)
+
+
+def butterflies(values):
+    values = list(values)
+    step = 1
+    while step < len(values):
+        for low in range(len(values)):
+            if low & step == 0:
+                first, second = values[low], values[low + step]
+                values[low], values[low + step] = first + second, first - second
+        step *= 2
+    return values
+
+
+def kernel(
+    n, x_hbm, g_hbm, weight, column_sign, row_sign, kept, q_hbm,
+    sk_ref, score_ref,
+    xs, gs, kb, wide_f32, tall_f32, turned, left, spread, out_box, in_box, total, q_box, skf, part, part_in,
+    x_sem, own_sem, q_sem, g_send, g_recv, r_send, r_recv, k_send, k_recv, p_send, p_recv, s_send, s_recv,
+):
+    me = lax.axis_index("wide")
+    core = lax.rem(me, 2)
+    chip = lax.div(me, 2)
+    partner = me + 1 - 2 * core
+    chips = n // 2
+    tokens = x_hbm.shape[0]
+    pair_tokens = 2 * tokens
+    width = n * g_hbm.shape[1]
+    cols = g_hbm.shape[1]
+    kept_dev = kept.shape[1]
+    row_blocks = width // ROWBLK
+    per_high = cols // ROWBLK
+    q_pieces = q_box.shape[0]
+    q_cols = q_box.shape[2]
+    scale = width**-0.5
+    mine = pl.ds(pl.multiple_of(core * tokens, tokens), tokens)
+
+    def remote(src, dst, send, recv, device):
+        return pltpu.make_async_remote_copy(
+            src_ref=src, dst_ref=dst, send_sem=send, recv_sem=recv,
+            device_id={"wide": device}, device_id_type=pl.DeviceIdType.MESH,
+        )
+
+    def grad_copy(source, device):
+        rows = pl.ds(pl.multiple_of(device * tokens, tokens), tokens)
+        half = pl.ds(pl.multiple_of(lax.rem(device, 2) * tokens, tokens), tokens)
+        return remote(g_hbm.at[rows, :], gs.at[source, half, :], g_send.at[device], g_recv.at[source], device)
+
+    def relay_copy(source):
+        return remote(gs.at[source, mine, :], gs.at[source, mine, :], r_send.at[source], r_recv.at[source], partner)
+
+    def kept_copy(source, device):
+        return remote(kept, kb.at[source], k_send.at[device], k_recv.at[source], device)
+
+    def part_copy(slot, source_chip, device):
+        return remote(out_box.at[slot], in_box.at[source_chip], p_send.at[slot], p_recv.at[source_chip], device)
+
+    def score_copy(source, device):
+        count = part_in.shape[1]
+        rows = pl.ds(pl.multiple_of(device * count, count), count)
+        return remote(part.at[rows, :], part_in.at[source], s_send.at[device], s_recv.at[source], device)
+
+    x_local = pltpu.make_async_copy(x_hbm, xs.at[mine, :], own_sem.at[0])
+    x_local.start()
+    own_rows = pl.ds(pl.multiple_of(me * tokens, tokens), tokens)
+    g_local = pltpu.make_async_copy(g_hbm.at[own_rows, :], gs.at[me, mine, :], own_sem.at[1])
+    g_local.start()
+
+    barrier = pltpu.get_barrier_semaphore()
+
+    @pl.loop(1, n)
+    def _(step):
+        pl.semaphore_signal(
+            barrier, inc=1, device_id={"wide": lax.rem(me + step, n)}, device_id_type=pl.DeviceIdType.MESH
+        )
+
+    pl.semaphore_wait(barrier, n - 1)
+
+    x_pair = remote(x_hbm, xs.at[mine, :], x_sem.at[0], x_sem.at[1], partner)
+    x_pair.start()
+
+    @pl.loop(1, n)
+    def _(step):
+        grad_copy(me, lax.rem(me + step, n)).start()
+
+    @pl.loop(1, chips)
+    def _(step):
+        kept_copy(me, lax.rem(me + 2 * step, n)).start()
+
+    def query_copy(piece):
+        begin = pl.multiple_of(piece * q_cols, q_cols)
+        return pltpu.make_async_copy(q_hbm.at[:, pl.ds(begin, q_cols)], q_box.at[piece], q_sem.at[piece])
+
+    @pl.loop(0, q_pieces)
+    def _(piece):
+        query_copy(piece).start()
+
+    kb[me] = kept[...]
+    table = signs(cols)
+    x_local.wait()
+    x_pair.wait()
+    token_weight = weight[...]
+    for block in range(n):
+        lanes = slice(block * cols, (block + 1) * cols)
+        signed = xs[:, lanes].astype(jnp.float32) * token_weight * column_sign[:, lanes].astype(jnp.float32)
+        wide_f32[block] = jnp.dot(signed.astype(jnp.bfloat16), table, preferred_element_type=jnp.float32)
+
+    @pl.loop(0, pair_tokens // 16)
+    def _(tile):
+        rows = pl.ds(pl.multiple_of(tile * 16, 16), 16)
+        for lane in range(0, cols, 128):
+            lanes = slice(lane, lane + 128)
+            mixed = butterflies([wide_f32[block, rows, lanes] for block in range(n)])
+            for block in range(n):
+                turned[block, rows, lanes] = (mixed[block] * scale).astype(jnp.bfloat16)
+
+    g_local.wait()
+    relay_copy(me).start()
+
+    @pl.loop(1, n)
+    def _(step):
+        source = lax.rem(me + n - step, n)
+        grad_copy(source, me).wait_recv()
+        relay_copy(source).start()
+
+    for block in range(n):
+        relay_copy(block).wait_recv()
+        lanes = slice(block * cols, (block + 1) * cols)
+        signed = (gs[block].astype(jnp.float32) * row_sign[:, lanes].astype(jnp.float32)).astype(jnp.bfloat16)
+        tall_f32[block] = lax.dot_general(
+            table, signed, (((1,), (1,)), ((), ())), preferred_element_type=jnp.float32
+        )
+
+    @pl.loop(0, cols // 16)
+    def _(tile):
+        rows = pl.ds(pl.multiple_of(tile * 16, 16), 16)
+        for lane in range(0, pair_tokens, 128):
+            lanes = slice(lane, lane + 128)
+            mixed = butterflies([tall_f32[block, rows, lanes] for block in range(n)])
+            for block in range(n):
+                begin = block * pair_tokens + lane
+                left[rows, begin : begin + 128] = (mixed[block] * scale).astype(jnp.bfloat16)
+
+    def contribution(device):
+        local = kb[device] - device * (cols * row_blocks)
+        column = jnp.right_shift(local, row_blocks.bit_length() - 1)
+        row = jnp.bitwise_and(local, row_blocks - 1)
+        high = jnp.right_shift(row, per_high.bit_length() - 1)
+        low = jnp.bitwise_and(row, per_high - 1)
+        hit = lax.broadcasted_iota(jnp.int32, (cols, kept_dev), 0) == column
+        chosen = jnp.dot(
+            turned[device],
+            jnp.where(hit, 1.0, 0.0).astype(jnp.bfloat16),
+            preferred_element_type=jnp.float32,
+        )
+        for block in range(n):
+            spread[block * pair_tokens : (block + 1) * pair_tokens, :] = jnp.where(high == block, chosen, 0.0).astype(
+                jnp.bfloat16
+            )
+        full = jnp.dot(left[...], spread[...], preferred_element_type=jnp.float32)
+        result = full[:ROWBLK]
+        for block in range(1, per_high):
+            result = jnp.where(low == block, full[block * ROWBLK : (block + 1) * ROWBLK], result)
+        return result
+
+    @pl.loop(1, chips)
+    def _(step):
+        target = lax.rem(me + 2 * step, n)
+        kept_copy(target, me).wait_recv()
+        out_box[step] = contribution(target).astype(jnp.bfloat16)
+        part_copy(step, chip, target).start()
+
+    total[...] = contribution(me)
+
+    @pl.loop(1, chips)
+    def _(step):
+        source = lax.rem(chip + chips - step, chips)
+        part_copy(step, source, me).wait_recv()
+        total[...] += in_box[source].astype(jnp.float32)
+
+    rounded = total[...].T.astype(jnp.bfloat16)
+    sk_ref[...] = rounded
+    skf[...] = rounded.astype(jnp.float32)
+    part[...] = jnp.zeros_like(part)
+    blocks_piece = q_cols // ROWBLK
+    group = 4
+    tall = 64
+
+    @pl.loop(0, q_pieces)
+    def _(piece):
+        query_copy(piece).wait()
+        for top in range(0, part.shape[0], tall):
+            def body(index, acc):
+                for extra in range(group):
+                    block = index * group + extra
+                    lanes = pl.ds(pl.multiple_of(block * ROWBLK, ROWBLK), ROWBLK)
+                    line = skf[pl.ds(piece * blocks_piece + block, 1), :]
+                    acc = acc + q_box[piece, top : top + tall, lanes].astype(jnp.float32) * line
+                return acc
+
+            part[top : top + tall, :] = lax.fori_loop(0, blocks_piece // group, body, part[top : top + tall, :])
+
+    @pl.loop(1, n)
+    def _(step):
+        score_copy(me, lax.rem(me + step, n)).start()
+
+    count = part_in.shape[1]
+    part_in[me] = part[pl.ds(pl.multiple_of(me * count, count), count), :]
+
+    @pl.loop(1, n)
+    def _(step):
+        score_copy(lax.rem(me + step, n), me).wait_recv()
+
+    summed = part_in[0]
+    for block in range(1, n):
+        summed = summed + part_in[block]
+    score_ref[...] = jnp.sum(summed, axis=1, keepdims=True)
+
+
+    @pl.loop(1, n)
+    def _(step):
+        device = lax.rem(me + step, n)
+        grad_copy(me, device).wait_send()
+        score_copy(me, device).wait_send()
+
+    @pl.loop(0, n)
+    def _(step):
+        relay_copy(step).wait_send()
+
+    @pl.loop(1, chips)
+    def _(step):
+        kept_copy(me, lax.rem(me + 2 * step, n)).wait_send()
+        part_copy(step, chip, lax.rem(me + 2 * step, n)).wait_send()
+
+
+def per_device(n, activations, output_grads, token_ids, row_signs, column_signs, kept_blocks, queries):
+    items, tokens, width = activations.shape
+    cols = output_grads.shape[2]
+    kept_dev = kept_blocks.shape[0]
+    nq = queries.shape[0]
+    q_pieces = 8
+    fits = (
+        items == 1
+        and n % 2 == 0
+        and n & (n - 1) == 0
+        and cols & (cols - 1) == 0
+        and cols % ROWBLK == 0
+        and tokens % 16 == 0
+        and (2 * tokens) % 128 == 0
+        and kept_dev % 128 == 0
+        and nq % (8 * n) == 0
+        and nq % 64 == 0
+        and kept_dev % (4 * q_pieces) == 0
+        and queries.size * 2 <= 2**25
+    )
+    if not fits:
+        return per_device_plain(
+            activations, output_grads, token_ids, row_signs, column_signs, kept_blocks, queries
+        )
+    chips = n // 2
+    chip = lax.div(lax.axis_index("wide"), 2)
+    ids = lax.dynamic_slice(token_ids[0], (chip * 2 * tokens,), (2 * tokens,))
+    weight = (ids != 0).astype(jnp.float32)[:, None]
+    bf16, f32 = jnp.bfloat16, jnp.float32
+    dma = pltpu.SemaphoreType.DMA
+    any_spec = pl.BlockSpec(memory_space=pl.ANY)
+    vmem_spec = pl.BlockSpec(memory_space=pltpu.VMEM)
+    sketches, scores = pl.pallas_call(
+        functools.partial(kernel, n),
+        out_shape=(
+            jax.ShapeDtypeStruct((kept_dev, ROWBLK), bf16),
+            jax.ShapeDtypeStruct((nq // n, 1), f32),
+        ),
+        in_specs=[any_spec, any_spec, vmem_spec, vmem_spec, vmem_spec, vmem_spec, any_spec],
+        out_specs=(vmem_spec, vmem_spec),
+        scratch_shapes=[
+            pltpu.VMEM((2 * tokens, width), bf16),
+            pltpu.VMEM((n, 2 * tokens, cols), bf16),
+            pltpu.VMEM((n, 1, kept_dev), jnp.int32),
+            pltpu.VMEM((n, 2 * tokens, cols), f32),
+            pltpu.VMEM((n, cols, 2 * tokens), f32),
+            pltpu.VMEM((n, 2 * tokens, cols), bf16),
+            pltpu.VMEM((cols, n * 2 * tokens), bf16),
+            pltpu.VMEM((n * 2 * tokens, kept_dev), bf16),
+            pltpu.VMEM((chips, ROWBLK, kept_dev), bf16),
+            pltpu.VMEM((chips, ROWBLK, kept_dev), bf16),
+            pltpu.VMEM((ROWBLK, kept_dev), f32),
+            pltpu.VMEM((q_pieces, nq, queries.shape[1] // q_pieces), bf16),
+            pltpu.VMEM((kept_dev, ROWBLK), f32),
+            pltpu.VMEM((nq, ROWBLK), f32),
+            pltpu.VMEM((n, nq // n, ROWBLK), f32),
+            dma((2,)), dma((2,)), dma((q_pieces,)),
+            dma((n,)), dma((n,)), dma((n,)), dma((n,)), dma((n,)), dma((n,)),
+            dma((chips,)), dma((chips,)), dma((n,)), dma((n,)),
+        ],
+        compiler_params=pltpu.CompilerParams(
+            collective_id=0, has_side_effects=True, vmem_limit_bytes=60 * 2**20
+        ),
+    )(
+        activations[0],
+        output_grads[0],
+        weight,
+        column_signs.astype(bf16)[None, :],
+        row_signs.astype(bf16)[None, :],
+        kept_blocks[None, :],
+        queries,
+    )
+    return sketches.reshape(1, kept_dev * ROWBLK), scores
+
+
 def solution(mesh):
     placed = (
         P("grp", "wide", None),
@@ -78,7 +402,7 @@
         P(None, "wide"),
     )
     return jax.shard_map(
-        per_device,
+        functools.partial(per_device, mesh.shape["wide"]),
         mesh=mesh,
         in_specs=placed,
         out_specs=(P("grp", "wide"), P("wide", "grp")),

time: 296 us -> 77.2 us (0.26)
  local copies, waits for them, and re-layouts: 106 us -> 5.05 us
  Pallas kernels: 0 us -> 69 us
  waiting for transfers between devices: 68.6 us -> 0 us
  matrix products: 51.7 us -> 0 us
  other arithmetic: 45.1 us -> 2.1 us
  between operations: 14.2 us -> 0.65 us
  starting transfers between devices: 7.7 us -> 0 us
    mul x4 -> x0, local copies, waits for them, and re-layouts: 87.5 us -> none  [the longest x1 87.2 us: hadamard_table(): high_table[:, None, :, None] * low_table[None, :, None, :]]
    pallas_call x0 -> x1, Pallas kernels: none -> 69 us  [per_device(): pl.pallas_call(functools.partial(kernel, n), out_shape=(jax.ShapeDtypeStr...]
    unnamed x3 -> x0, waiting for transfers between devices: 55 us -> none
    dot_general x3 -> x0, matrix products: 51.7 us -> none  [the longest x1 22.9 us: per_device(): jnp.einsum('scj,ji->sci', signed, hadamard, preferred_element_type=jnp.fl...]
    unnamed x1 -> x0, other arithmetic: 22.4 us -> none
    mul x3 -> x0, other arithmetic: 21.4 us -> none  [the longest x1 21.2 us: hadamard_table(): high_table[:, None, :, None] * low_table[None, :, None, :]]
    all_to_all x1 -> x0, waiting for transfers between devices: 13.6 us -> none  [per_device(): lax.all_to_all(turned, 'wide', split_axis=2, concat_axis=1, tiled=True)]
    all_to_all x1 -> x0, starting transfers between devices: 7.44 us -> none  [per_device(): lax.all_to_all(turned, 'wide', split_axis=2, concat_axis=1, tiled=True)]
  transfers between devices with their start and end apart: 3 -> 0, of which waited for: 2 -> 0; matrix products, arithmetic and copies ran while one was open for 53% -> 0% of each run, Pallas kernels for 0% -> 0%
where the time goes in v1:
time: 77.2 us; the launch traced here: 76.8 us
  Pallas kernels  69 us (89%)
  local copies, waits for them, and re-layouts  5.05 us (7%)
  other arithmetic  2.1 us (3%)
    pallas_call x1, Pallas kernels, per_device(): pl.pallas_call(functools.partial(kernel, n), out_shape=(jax.ShapeDtypeStr...  69 us
    unnamed x2, local copies, waits for them, and re-layouts  3.09 us

profile of v1, /device:TPU:0, one launch (start us, length us, event | category | flops | bytes accessed | tf_op | source)
XLA Modules:
  0.0 76.8 jit_solution(6056792543164278421)
XLA Ops:
  0.6 0.7 fusion
  1.3 0.7 convert_element_type.22
  2.0 0.6 broadcast_in_dim.11.row_sign
  2.6 0.7 convert_element_type.21
  3.4 0.6 broadcast_in_dim.10.column_sign
  4.0 0.7 copy.9.weight
  4.7 69.0 %shard_map.86 = (bf16[512,128]{1,0:T(8,128)(2,1)}, f32[16,1]{1,0:T(8,128)}) custom-call(bf16[64,4096]{1,0:T(8,128)(2,1)} %bitcast.10, bf16[1024,256]{1,0:T(8,128)(2,1)} %bitcast.11, f32[128,1]{1,0:T(8,128)} %copy.9.weight, bf16[1,4096]{1,0:T(2,128)(2,1)} %broadcast_in_dim.10.column_sign, bf16[1,4096]{1,0:T(2,128)(2,1)} %broadcast_in_dim.11.row_sign, ...), custom_call_target="tpu_custom_call" | custom-call | tf_op jit(solution)/shard_map/pallas_call | solution.py:351
  73.7 1.3 %copy.10 = f32[16,1]{0,1:T(1,128)} copy(f32[16,1]{1,0:T(8,128)} %get-tuple-element.7) | data formatting | bytes 128
  75.0 1.8 %copy.13 = bf16[1,1,512,128]{3,1,2,0:T(2,128)(2,1)} copy(bf16[1,1,512,128]{3,2,1,0:T(8,128)(2,1)} %bitcast.13) | data formatting | bytes 262144

commit v2 on v1

--- a/solution.py
+++ b/solution.py
@@ -96,10 +96,10 @@
 
 
 def kernel(
-    n, x_hbm, g_hbm, weight, column_sign, row_sign, kept, q_hbm,
+    n, x_hbm, g_hbm, ids, column_sign, row_sign, kept, q_hbm,
     sk_ref, score_ref,
-    xs, gs, kb, wide_f32, tall_f32, turned, left, spread, out_box, in_box, total, q_box, skf, part, part_in,
-    x_sem, own_sem, q_sem, g_send, g_recv, r_send, r_recv, k_send, k_recv, p_send, p_recv, s_send, s_recv,
+    xs, gs, kb, wide_f32, tall_f32, turned, left, spread, out_a, in_a, out_b, in_b, total, q_box, skf, part, part_in,
+    x_sem, own_sem, q_sem, g_send, g_recv, r_send, r_recv, k_send, k_recv, a_send, a_recv, b_send, b_recv, s_send, s_recv,
 ):
     me = lax.axis_index("wide")
     core = lax.rem(me, 2)
@@ -110,7 +110,10 @@
     pair_tokens = 2 * tokens
     width = n * g_hbm.shape[1]
     cols = g_hbm.shape[1]
-    kept_dev = kept.shape[1]
+    kept_dev = kept.shape[0] * kept.shape[1]
+    levels = chips // 2
+    side = lax.rem(chip, 2)
+    level = lax.div(chip, 2)
     row_blocks = width // ROWBLK
     per_high = cols // ROWBLK
     q_pieces = q_box.shape[0]
@@ -135,13 +138,17 @@
     def kept_copy(source, device):
         return remote(kept, kb.at[source], k_send.at[device], k_recv.at[source], device)
 
-    def part_copy(slot, source_chip, device):
-        return remote(out_box.at[slot], in_box.at[source_chip], p_send.at[slot], p_recv.at[source_chip], device)
+    def target(to_level, to_side):
+        return 4 * to_level + 2 * to_side + core
+
+    def cross_copy(at):
+        return remote(out_a.at[at], in_a.at[at], a_send.at[at], a_recv.at[at], target(level, 1 - side))
+
+    def down_copy(source, at):
+        return remote(out_b.at[at], in_b.at[source], b_send.at[at], b_recv.at[source], target(at, side))
 
     def score_copy(source, device):
-        count = part_in.shape[1]
-        rows = pl.ds(pl.multiple_of(device * count, count), count)
-        return remote(part.at[rows, :], part_in.at[source], s_send.at[device], s_recv.at[source], device)
+        return remote(part, part_in.at[source], s_send.at[device], s_recv.at[source], device)
 
     x_local = pltpu.make_async_copy(x_hbm, xs.at[mine, :], own_sem.at[0])
     x_local.start()
@@ -180,13 +187,35 @@
 
     kb[me] = kept[...]
     table = signs(cols)
-    x_local.wait()
-    x_pair.wait()
-    token_weight = weight[...]
-    for block in range(n):
-        lanes = slice(block * cols, (block + 1) * cols)
-        signed = xs[:, lanes].astype(jnp.float32) * token_weight * column_sign[:, lanes].astype(jnp.float32)
+
+    def sign_row(signs_ref, block):
+        per = cols // 128
+        rows = [signs_ref[pl.ds(block * per + extra, 1), :] for extra in range(per)]
+        return jnp.concatenate(rows, axis=1).astype(jnp.float32)
+
+    def turn_block(block):
+        lanes = pl.ds(pl.multiple_of(block * cols, cols), cols)
+        signed = xs[:, lanes].astype(jnp.float32) * sign_row(column_sign, block)
         wide_f32[block] = jnp.dot(signed.astype(jnp.bfloat16), table, preferred_element_type=jnp.float32)
+
+    g_local.wait()
+    relay_copy(me).start()
+
+    @pl.loop(1, n)
+    def _(step):
+        source = lax.rem(me + n - step, n)
+        grad_copy(source, me).wait_recv()
+        relay_copy(source).start()
+
+        @pl.when(step == n // 2)
+        def _():
+            x_local.wait()
+            x_pair.wait()
+
+        @pl.when(step >= n // 2)
+        def _():
+            turn_block(2 * step - n)
+            turn_block(2 * step - n + 1)
 
     @pl.loop(0, pair_tokens // 16)
     def _(tile):
@@ -197,19 +226,12 @@
             for block in range(n):
                 turned[block, rows, lanes] = (mixed[block] * scale).astype(jnp.bfloat16)
 
-    g_local.wait()
-    relay_copy(me).start()
-
-    @pl.loop(1, n)
-    def _(step):
-        source = lax.rem(me + n - step, n)
-        grad_copy(source, me).wait_recv()
-        relay_copy(source).start()
+    token_row = ids[:, pl.ds(pl.multiple_of(chip * pair_tokens, pair_tokens), pair_tokens)]
+    weight = jnp.where(token_row != 0, scale, 0.0).astype(jnp.float32)
 
     for block in range(n):
         relay_copy(block).wait_recv()
-        lanes = slice(block * cols, (block + 1) * cols)
-        signed = (gs[block].astype(jnp.float32) * row_sign[:, lanes].astype(jnp.float32)).astype(jnp.bfloat16)
+        signed = (gs[block].astype(jnp.float32) * sign_row(row_sign, block)).astype(jnp.bfloat16)
         tall_f32[block] = lax.dot_general(
             table, signed, (((1,), (1,)), ((), ())), preferred_element_type=jnp.float32
         )
@@ -222,10 +244,12 @@
             mixed = butterflies([tall_f32[block, rows, lanes] for block in range(n)])
             for block in range(n):
                 begin = block * pair_tokens + lane
-                left[rows, begin : begin + 128] = (mixed[block] * scale).astype(jnp.bfloat16)
+                left[rows, begin : begin + 128] = (mixed[block] * weight[:, lanes]).astype(jnp.bfloat16)
 
     def contribution(device):
-        local = kb[device] - device * (cols * row_blocks)
+        rows = kb[device]
+        local = jnp.concatenate([rows[at : at + 1] for at in range(rows.shape[0])], axis=1)
+        local = local - device * (cols * row_blocks)
         column = jnp.right_shift(local, row_blocks.bit_length() - 1)
         row = jnp.bitwise_and(local, row_blocks - 1)
         high = jnp.right_shift(row, per_high.bit_length() - 1)
@@ -246,49 +270,77 @@
             result = jnp.where(low == block, full[block * ROWBLK : (block + 1) * ROWBLK], result)
         return result
 
-    @pl.loop(1, chips)
-    def _(step):
-        target = lax.rem(me + 2 * step, n)
-        kept_copy(target, me).wait_recv()
-        out_box[step] = contribution(target).astype(jnp.bfloat16)
-        part_copy(step, chip, target).start()
-
-    total[...] = contribution(me)
-
-    @pl.loop(1, chips)
-    def _(step):
-        source = lax.rem(chip + chips - step, chips)
-        part_copy(step, source, me).wait_recv()
-        total[...] += in_box[source].astype(jnp.float32)
+    @pl.loop(0, levels + 1)
+    def _(step):
+        @pl.when(step < levels)
+        def _():
+            at = lax.rem(level + 1 + step, levels)
+            device = target(at, 1 - side)
+            kept_copy(device, me).wait_recv()
+            out_a[at] = contribution(device).astype(jnp.bfloat16)
+            cross_copy(at).start()
+
+        @pl.when(step >= 1)
+        def _():
+            at = lax.rem(level + step, levels)
+            device = target(at, side)
+
+            @pl.when(step < levels)
+            def _():
+                kept_copy(device, me).wait_recv()
+
+            total[...] = contribution(device)
+            cross_copy(at).wait_recv()
+
+            @pl.when(step < levels)
+            def _():
+                out_b[at] = (total[...] + in_a[at].astype(jnp.float32)).astype(jnp.bfloat16)
+                down_copy(level, at).start()
+
+    total[...] += in_a[level].astype(jnp.float32)
+
+    @pl.loop(1, levels)
+    def _(step):
+        source = lax.rem(level + levels - step, levels)
+        down_copy(source, level).wait_recv()
+        total[...] += in_b[source].astype(jnp.float32)
 
     rounded = total[...].T.astype(jnp.bfloat16)
     sk_ref[...] = rounded
     skf[...] = rounded.astype(jnp.float32)
-    part[...] = jnp.zeros_like(part)
     blocks_piece = q_cols // ROWBLK
     group = 4
-    tall = 64
-
-    @pl.loop(0, q_pieces)
-    def _(piece):
+
+    def piece_scores(piece, acc):
         query_copy(piece).wait()
-        for top in range(0, part.shape[0], tall):
-            def body(index, acc):
-                for extra in range(group):
-                    block = index * group + extra
-                    lanes = pl.ds(pl.multiple_of(block * ROWBLK, ROWBLK), ROWBLK)
-                    line = skf[pl.ds(piece * blocks_piece + block, 1), :]
-                    acc = acc + q_box[piece, top : top + tall, lanes].astype(jnp.float32) * line
-                return acc
-
-            part[top : top + tall, :] = lax.fori_loop(0, blocks_piece // group, body, part[top : top + tall, :])
+
+        def body(index, acc):
+            for extra in range(group):
+                block = (index * group + extra) * 2
+                lanes = pl.ds(pl.multiple_of(block * ROWBLK, 2 * ROWBLK), 2 * ROWBLK)
+                line = [
+                    jnp.broadcast_to(skf[pl.ds(piece * blocks_piece + block + at, 1), :], (16, ROWBLK))
+                    for at in range(2)
+                ]
+                acc = acc + lax.dot_general(
+                    jnp.concatenate(line, axis=1).astype(jnp.bfloat16),
+                    q_box[piece, :, lanes],
+                    (((1,), (1,)), ((), ())),
+                    preferred_element_type=jnp.float32,
+                )
+            return acc
+
+        return lax.fori_loop(0, blocks_piece // (2 * group), body, acc)
+
+    nq = q_hbm.shape[0]
+    acc = lax.fori_loop(0, q_pieces, piece_scores, jnp.zeros((16, nq), jnp.float32))
+    part[...] = acc[:8]
 
     @pl.loop(1, n)
     def _(step):
         score_copy(me, lax.rem(me + step, n)).start()
 
-    count = part_in.shape[1]
-    part_in[me] = part[pl.ds(pl.multiple_of(me * count, count), count), :]
+    part_in[me] = acc[:8]
 
     @pl.loop(1, n)
     def _(step):
@@ -297,8 +349,10 @@
     summed = part_in[0]
     for block in range(1, n):
         summed = summed + part_in[block]
-    score_ref[...] = jnp.sum(summed, axis=1, keepdims=True)
-
+    count = score_ref.shape[0]
+    spot = lax.broadcasted_iota(jnp.int32, (count, nq), 0) + me * count
+    own = lax.broadcasted_iota(jnp.int32, (count, nq), 1) == spot
+    score_ref[...] = jnp.sum(jnp.where(own, summed[:1], 0.0), axis=1, keepdims=True)
 
     @pl.loop(1, n)
     def _(step):
@@ -313,7 +367,14 @@
     @pl.loop(1, chips)
     def _(step):
         kept_copy(me, lax.rem(me + 2 * step, n)).wait_send()
-        part_copy(step, chip, lax.rem(me + 2 * step, n)).wait_send()
+
+    @pl.loop(0, levels)
+    def _(step):
+        cross_copy(step).wait_send()
+
+    @pl.loop(1, levels)
+    def _(step):
+        down_copy(level, lax.rem(level + step, levels)).wait_send()
 
 
 def per_device(n, activations, output_grads, token_ids, row_signs, column_signs, kept_blocks, queries):
@@ -324,7 +385,7 @@
     q_pieces = 8
     fits = (
         items == 1
-        and n % 2 == 0
+        and n % 4 == 0
         and n & (n - 1) == 0
         and cols & (cols - 1) == 0
         and cols % ROWBLK == 0
@@ -333,7 +394,7 @@
         and kept_dev % 128 == 0
         and nq % (8 * n) == 0
         and nq % 64 == 0
-        and kept_dev % (4 * q_pieces) == 0
+        and kept_dev % (8 * q_pieces) == 0
         and queries.size * 2 <= 2**25
     )
     if not fits:
@@ -341,9 +402,6 @@
             activations, output_grads, token_ids, row_signs, column_signs, kept_blocks, queries
         )
     chips = n // 2
-    chip = lax.div(lax.axis_index("wide"), 2)
-    ids = lax.dynamic_slice(token_ids[0], (chip * 2 * tokens,), (2 * tokens,))
-    weight = (ids != 0).astype(jnp.float32)[:, None]
     bf16, f32 = jnp.bfloat16, jnp.float32
     dma = pltpu.SemaphoreType.DMA
     any_spec = pl.BlockSpec(memory_space=pl.ANY)
@@ -359,22 +417,24 @@
         scratch_shapes=[
             pltpu.VMEM((2 * tokens, width), bf16),
             pltpu.VMEM((n, 2 * tokens, cols), bf16),
-            pltpu.VMEM((n, 1, kept_dev), jnp.int32),
+            pltpu.VMEM((n, kept_dev // 128, 128), jnp.int32),
             pltpu.VMEM((n, 2 * tokens, cols), f32),
             pltpu.VMEM((n, cols, 2 * tokens), f32),
             pltpu.VMEM((n, 2 * tokens, cols), bf16),
             pltpu.VMEM((cols, n * 2 * tokens), bf16),
             pltpu.VMEM((n * 2 * tokens, kept_dev), bf16),
-            pltpu.VMEM((chips, ROWBLK, kept_dev), bf16),
-            pltpu.VMEM((chips, ROWBLK, kept_dev), bf16),
+            pltpu.VMEM((chips // 2, ROWBLK, kept_dev), bf16),
+            pltpu.VMEM((chips // 2, ROWBLK, kept_dev), bf16),
+            pltpu.VMEM((chips // 2, ROWBLK, kept_dev), bf16),
+            pltpu.VMEM((chips // 2, ROWBLK, kept_dev), bf16),
             pltpu.VMEM((ROWBLK, kept_dev), f32),
             pltpu.VMEM((q_pieces, nq, queries.shape[1] // q_pieces), bf16),
             pltpu.VMEM((kept_dev, ROWBLK), f32),
-            pltpu.VMEM((nq, ROWBLK), f32),
-            pltpu.VMEM((n, nq // n, ROWBLK), f32),
+            pltpu.VMEM((8, nq), f32),
+            pltpu.VMEM((n, 8, nq), f32),
             dma((2,)), dma((2,)), dma((q_pieces,)),
             dma((n,)), dma((n,)), dma((n,)), dma((n,)), dma((n,)), dma((n,)),
-            dma((chips,)), dma((chips,)), dma((n,)), dma((n,)),
+            dma((chips // 2,)), dma((chips // 2,)), dma((chips // 2,)), dma((chips // 2,)), dma((n,)), dma((n,)),
         ],
         compiler_params=pltpu.CompilerParams(
             collective_id=0, has_side_effects=True, vmem_limit_bytes=60 * 2**20
@@ -382,10 +442,10 @@
     )(
         activations[0],
         output_grads[0],
-        weight,
-        column_signs.astype(bf16)[None, :],
-        row_signs.astype(bf16)[None, :],
-        kept_blocks[None, :],
+        token_ids,
+        column_signs.reshape(-1, 128),
+        row_signs.reshape(-1, 128),
+        kept_blocks.reshape(-1, 128),
         queries,
     )
     return sketches.reshape(1, kept_dev * ROWBLK), scores

time: 77.2 us -> 70 us (0.907)
  Pallas kernels: 69 us -> 66 us
  other arithmetic: 2.1 us -> 0 us
  local copies, waits for them, and re-layouts: 5.05 us -> 3.09 us
    pallas_call x1, Pallas kernels: 69 us -> 66 us  [per_device(): pl.pallas_call(functools.partial(kernel, n), out_shape=(jax.ShapeDtypeStr...]
    convert_element_type x3 -> x0, other arithmetic: 2.1 us -> none  [the longest x1 0.72 us: per_device(): row_signs.astype(bf16)[None, :]]
    broadcast_in_dim x2 -> x0, local copies, waits for them, and re-layouts: 1.22 us -> none  [the longest x1 0.61 us: per_device(): row_signs.astype(bf16)[None, :]]
where the time goes in v2:
time: 70 us; the launch traced here: 69.7 us
  Pallas kernels  66 us (94%)
  local copies, waits for them, and re-layouts  3.09 us (4%)
    pallas_call x1, Pallas kernels, per_device(): pl.pallas_call(functools.partial(kernel, n), out_shape=(jax.ShapeDtypeStr...  66 us
    unnamed x2, local copies, waits for them, and re-layouts  3.09 us

profile of v2, /device:TPU:0, one launch (start us, length us, event | category | flops | bytes accessed | tf_op | source)
XLA Modules:
  0.0 69.7 jit_solution(14501869205672308942)
XLA Ops:
  0.6 66.0 %shard_map.86 = (bf16[512,128]{1,0:T(8,128)(2,1)}, f32[16,1]{1,0:T(8,128)}) custom-call(bf16[64,4096]{1,0:T(8,128)(2,1)} %bitcast.10, bf16[1024,256]{1,0:T(8,128)(2,1)} %bitcast.11, s32[1,1024]{1,0:T(1,128)} %ids.1, s32[32,128]{1,0:T(8,128)} %bitcast.14, s32[32,128]{1,0:T(8,128)} %bitcast.15, s32[4,128]{1,0:T(4,128)} %bitcast.16, bf16[256,65536]{1,0:T(8,128)(2,1)} %q_hbm.1), custom_call_target="tpu_custom_call" | custom-call | tf_op jit(solution)/shard_map/pallas_call | solution.py:409
  66.6 1.3 %copy.9 = f32[16,1]{0,1:T(1,128)} copy(f32[16,1]{1,0:T(8,128)} %get-tuple-element.7) | data formatting | bytes 128
  67.9 1.8 %copy.12 = bf16[1,1,512,128]{3,1,2,0:T(2,128)(2,1)} copy(bf16[1,1,512,128]{3,2,1,0:T(8,128)(2,1)} %bitcast.13) | data formatting | bytes 262144

commit v3 on v2

--- a/solution.py
+++ b/solution.py
@@ -309,38 +309,42 @@
     sk_ref[...] = rounded
     skf[...] = rounded.astype(jnp.float32)
     blocks_piece = q_cols // ROWBLK
-    group = 4
-
-    def piece_scores(piece, acc):
+    nq = q_hbm.shape[0]
+
+    def line_of(piece, block):
+        line = skf[pl.ds(piece * blocks_piece + block, 1), :]
+        return jnp.broadcast_to(line, (16, ROWBLK))[None]
+
+    def piece_scores(piece, accs):
         query_copy(piece).wait()
 
-        def body(index, acc):
-            for extra in range(group):
-                block = (index * group + extra) * 2
-                lanes = pl.ds(pl.multiple_of(block * ROWBLK, 2 * ROWBLK), 2 * ROWBLK)
-                line = [
-                    jnp.broadcast_to(skf[pl.ds(piece * blocks_piece + block + at, 1), :], (16, ROWBLK))
-                    for at in range(2)
-                ]
-                acc = acc + lax.dot_general(
-                    jnp.concatenate(line, axis=1).astype(jnp.bfloat16),
-                    q_box[piece, :, lanes],
-                    (((1,), (1,)), ((), ())),
-                    preferred_element_type=jnp.float32,
-                )
-            return acc
-
-        return lax.fori_loop(0, blocks_piece // (2 * group), body, acc)
-
-    nq = q_hbm.shape[0]
-    acc = lax.fori_loop(0, q_pieces, piece_scores, jnp.zeros((16, nq), jnp.float32))
-    part[...] = acc[:8]
+        def body(index, accs):
+            accs = list(accs)
+            for extra in range(4):
+                block = (index * 4 + extra) * 2
+                lines = [line_of(piece, block + at) for at in range(2)]
+                for top in range(0, nq, 64):
+                    both = None
+                    for at in range(2):
+                        lanes = pl.ds(pl.multiple_of((block + at) * ROWBLK, ROWBLK), ROWBLK)
+                        rows = q_box[piece, top : top + 64, lanes].reshape(64 // 16, 16, ROWBLK)
+                        term = rows.astype(jnp.float32) * lines[at]
+                        both = term if both is None else both + term
+                    accs[top // 64] += both.reshape(64, ROWBLK).astype(jnp.float32)
+            return tuple(accs)
+
+        return lax.fori_loop(0, blocks_piece // (2 * 4), body, accs)
+
+    zeros = tuple(jnp.zeros((64, ROWBLK), jnp.float32) for _ in range(nq // 64))
+    accs = lax.fori_loop(0, q_pieces, piece_scores, zeros)
+    columns = jnp.concatenate(accs, axis=0).T
+    part[...] = jnp.sum(columns, axis=0, keepdims=True)
 
     @pl.loop(1, n)
     def _(step):
         score_copy(me, lax.rem(me + step, n)).start()
 
-    part_in[me] = acc[:8]
+    part_in[me] = part[...]
 
     @pl.loop(1, n)
     def _(step):
@@ -349,10 +353,11 @@
     summed = part_in[0]
     for block in range(1, n):
         summed = summed + part_in[block]
-    count = score_ref.shape[0]
-    spot = lax.broadcasted_iota(jnp.int32, (count, nq), 0) + me * count
-    own = lax.broadcasted_iota(jnp.int32, (count, nq), 1) == spot
-    score_ref[...] = jnp.sum(jnp.where(own, summed[:1], 0.0), axis=1, keepdims=True)
+    count = score_ref.shape[1]
+    spot = lax.broadcasted_iota(jnp.int32, (128, nq), 0) + me * count
+    own = lax.broadcasted_iota(jnp.int32, (128, nq), 1) == spot
+    column = jnp.sum(jnp.where(own, summed, 0.0), axis=1, keepdims=True)
+    score_ref[...] = jnp.broadcast_to(column, (128, 128)).T[:1, :count]
 
     @pl.loop(1, n)
     def _(step):
@@ -394,6 +399,7 @@
         and kept_dev % 128 == 0
         and nq % (8 * n) == 0
         and nq % 64 == 0
+        and nq // n <= 128
         and kept_dev % (8 * q_pieces) == 0
         and queries.size * 2 <= 2**25
     )
@@ -410,7 +416,7 @@
         functools.partial(kernel, n),
         out_shape=(
             jax.ShapeDtypeStruct((kept_dev, ROWBLK), bf16),
-            jax.ShapeDtypeStruct((nq // n, 1), f32),
+            jax.ShapeDtypeStruct((1, nq // n), f32),
         ),
         in_specs=[any_spec, any_spec, vmem_spec, vmem_spec, vmem_spec, vmem_spec, any_spec],
         out_specs=(vmem_spec, vmem_spec),
@@ -430,8 +436,8 @@
             pltpu.VMEM((ROWBLK, kept_dev), f32),
             pltpu.VMEM((q_pieces, nq, queries.shape[1] // q_pieces), bf16),
             pltpu.VMEM((kept_dev, ROWBLK), f32),
-            pltpu.VMEM((8, nq), f32),
-            pltpu.VMEM((n, 8, nq), f32),
+            pltpu.VMEM((1, nq), f32),
+            pltpu.VMEM((n, 1, nq), f32),
             dma((2,)), dma((2,)), dma((q_pieces,)),
             dma((n,)), dma((n,)), dma((n,)), dma((n,)), dma((n,)), dma((n,)),
             dma((chips // 2,)), dma((chips // 2,)), dma((chips // 2,)), dma((chips // 2,)), dma((n,)), dma((n,)),
@@ -448,7 +454,7 @@
         kept_blocks.reshape(-1, 128),
         queries,
     )
-    return sketches.reshape(1, kept_dev * ROWBLK), scores
+    return sketches.reshape(1, kept_dev * ROWBLK), scores.reshape(nq // n, 1)
 
 
 def solution(mesh):

time: 70 us -> 63.1 us (0.901)
  Pallas kernels: 66 us -> 59.2 us
    pallas_call x1, Pallas kernels: 66 us -> 59.2 us  [per_device(): pl.pallas_call(functools.partial(kernel, n), out_shape=(jax.ShapeDtypeStr...]
where the time goes in v3:
time: 63.1 us; the launch traced here: 62.8 us
  Pallas kernels  59.2 us (94%)
  local copies, waits for them, and re-layouts  2.98 us (5%)
  between operations  0.64 us (1%)
    pallas_call x1, Pallas kernels, per_device(): pl.pallas_call(functools.partial(kernel, n), out_shape=(jax.ShapeDtypeStr...  59.2 us
    unnamed x2, local copies, waits for them, and re-layouts  2.98 us

profile of v3, /device:TPU:0, one launch (start us, length us, event | category | flops | bytes accessed | tf_op | source)
XLA Modules:
  0.0 62.8 jit_solution(12858733206753661508)
XLA Ops:
  0.6 59.2 %shard_map.86 = (bf16[512,128]{1,0:T(8,128)(2,1)}, f32[1,16]{1,0:T(1,128)}) custom-call(bf16[64,4096]{1,0:T(8,128)(2,1)} %bitcast.11, bf16[1024,256]{1,0:T(8,128)(2,1)} %bitcast.12, s32[1,1024]{1,0:T(1,128)} %ids.1, s32[32,128]{1,0:T(8,128)} %bitcast.15, s32[32,128]{1,0:T(8,128)} %bitcast.16, s32[4,128]{1,0:T(4,128)} %bitcast.17, bf16[256,65536]{1,0:T(8,128)(2,1)} %q_hbm.1), custom_call_target="tpu_custom_call" | custom-call | tf_op jit(solution)/shard_map/pallas_call | solution.py:415
  59.8 1.8 %copy.11 = bf16[1,1,512,128]{3,1,2,0:T(2,128)(2,1)} copy(bf16[1,1,512,128]{3,2,1,0:T(8,128)(2,1)} %bitcast.14) | data formatting | bytes 262144
  61.6 1.2 %copy.13 = f32[16,1]{0,1:T(1,128)} copy(f32[16,1]{0,1:T(1,128)} %bitcast.18) | data formatting | bytes 128

commit v4 on v3

--- a/solution.py
+++ b/solution.py
@@ -191,12 +191,12 @@
     def sign_row(signs_ref, block):
         per = cols // 128
         rows = [signs_ref[pl.ds(block * per + extra, 1), :] for extra in range(per)]
-        return jnp.concatenate(rows, axis=1).astype(jnp.float32)
+        return jnp.concatenate(rows, axis=1).astype(jnp.float32).astype(jnp.bfloat16)
 
     def turn_block(block):
         lanes = pl.ds(pl.multiple_of(block * cols, cols), cols)
-        signed = xs[:, lanes].astype(jnp.float32) * sign_row(column_sign, block)
-        wide_f32[block] = jnp.dot(signed.astype(jnp.bfloat16), table, preferred_element_type=jnp.float32)
+        signed = xs[:, lanes] * sign_row(column_sign, block)
+        wide_f32[block] = jnp.dot(signed, table, preferred_element_type=jnp.float32)
 
     g_local.wait()
     relay_copy(me).start()
@@ -231,7 +231,7 @@
 
     for block in range(n):
         relay_copy(block).wait_recv()
-        signed = (gs[block].astype(jnp.float32) * sign_row(row_sign, block)).astype(jnp.bfloat16)
+        signed = gs[block] * sign_row(row_sign, block)
         tall_f32[block] = lax.dot_general(
             table, signed, (((1,), (1,)), ((), ())), preferred_element_type=jnp.float32
         )
@@ -260,10 +260,10 @@
             jnp.where(hit, 1.0, 0.0).astype(jnp.bfloat16),
             preferred_element_type=jnp.float32,
         )
+        chosen = chosen.astype(jnp.bfloat16)
         for block in range(n):
-            spread[block * pair_tokens : (block + 1) * pair_tokens, :] = jnp.where(high == block, chosen, 0.0).astype(
-                jnp.bfloat16
-            )
+            keep = jnp.where(high == block, 1.0, 0.0).astype(jnp.bfloat16)
+            spread[block * pair_tokens : (block + 1) * pair_tokens, :] = chosen * keep
         full = jnp.dot(left[...], spread[...], preferred_element_type=jnp.float32)
         result = full[:ROWBLK]
         for block in range(1, per_high):
@@ -320,8 +320,8 @@
 
         def body(index, accs):
             accs = list(accs)
-            for extra in range(4):
-                block = (index * 4 + extra) * 2
+            for extra in range(8):
+                block = (index * 8 + extra) * 2
                 lines = [line_of(piece, block + at) for at in range(2)]
                 for top in range(0, nq, 64):
                     both = None
@@ -333,7 +333,7 @@
                     accs[top // 64] += both.reshape(64, ROWBLK).astype(jnp.float32)
             return tuple(accs)
 
-        return lax.fori_loop(0, blocks_piece // (2 * 4), body, accs)
+        return lax.fori_loop(0, blocks_piece // (2 * 8), body, accs)
 
     zeros = tuple(jnp.zeros((64, ROWBLK), jnp.float32) for _ in range(nq // 64))
     accs = lax.fori_loop(0, q_pieces, piece_scores, zeros)
@@ -400,7 +400,7 @@
         and nq % (8 * n) == 0
         and nq % 64 == 0
         and nq // n <= 128
-        and kept_dev % (8 * q_pieces) == 0
+        and kept_dev % (16 * q_pieces) == 0
         and queries.size * 2 <= 2**25
     )
     if not fits:

time: 63.1 us -> 62.8 us (level)
  no operation moved by 1% of the time
where the time goes in v4:
time: 62.8 us; the launch traced here: 62.5 us
  Pallas kernels  58.9 us (94%)
  local copies, waits for them, and re-layouts  2.98 us (5%)
  between operations  0.64 us (1%)
    pallas_call x1, Pallas kernels, per_device(): pl.pallas_call(functools.partial(kernel, n), out_shape=(jax.ShapeDtypeStr...  58.9 us
    unnamed x2, local copies, waits for them, and re-layouts  2.98 us

profile of v4, /device:TPU:0, one launch (start us, length us, event | category | flops | bytes accessed | tf_op | source)
XLA Modules:
  0.0 62.5 jit_solution(15133414874809114595)
XLA Ops:
  0.6 58.9 %shard_map.86 = (bf16[512,128]{1,0:T(8,128)(2,1)}, f32[1,16]{1,0:T(1,128)}) custom-call(bf16[64,4096]{1,0:T(8,128)(2,1)} %bitcast.11, bf16[1024,256]{1,0:T(8,128)(2,1)} %bitcast.12, s32[1,1024]{1,0:T(1,128)} %ids.1, s32[32,128]{1,0:T(8,128)} %bitcast.15, s32[32,128]{1,0:T(8,128)} %bitcast.16, s32[4,128]{1,0:T(4,128)} %bitcast.17, bf16[256,65536]{1,0:T(8,128)(2,1)} %q_hbm.1), custom_call_target="tpu_custom_call" | custom-call | tf_op jit(solution)/shard_map/pallas_call | solution.py:415
  59.5 1.8 %copy.11 = bf16[1,1,512,128]{3,1,2,0:T(2,128)(2,1)} copy(bf16[1,1,512,128]{3,2,1,0:T(8,128)(2,1)} %bitcast.14) | data formatting | bytes 262144
  61.3 1.2 %copy.13 = f32[16,1]{0,1:T(1,128)} copy(f32[16,1]{0,1:T(1,128)} %bitcast.18) | data formatting | bytes 128
